TPU v7x, 32 devices: a whole 2x2x4 slice. The times are simulated.
32 devices in a mesh: fsdp: 4 (over y, x), rep: 8 (over z, core).
Axes of the slice: x: 2, y: 2, z: 4, core: 2. Of those that a mesh axis runs over, the one named last changes fastest.
Arguments:
- tokens: bfloat16 [64, 256, 384], P(('fsdp', 'rep')), may hold values from -6 to 6
- conditions: bfloat16 [64, 384], P(('fsdp', 'rep')), may hold values from -6 to 6
- assignment: int32 [64], P(('fsdp', 'rep')), may hold values from 0 to 63, each once
- params: float32 [2654208], P('fsdp')
- momentum: float32 [2654208], P('fsdp'), may hold values from -24 to 24
- cotangent: bfloat16 [64, 256, 384], P(('fsdp', 'rep')), may hold values from -6 to 6
Outputs:
- blended: bfloat16 [64, 256, 384], P(('fsdp', 'rep'))
- grad_tokens: float32 [64, 256, 384], P(('fsdp', 'rep'))
- grad_params: float32 [2654208], P('fsdp')
- new_params: float32 [2654208], P('fsdp')
- new_momentum: float32 [2654208], P('fsdp')
Inputs may be any that keep to these rules, and one draw needn't show every extreme that they name: assignment is a permutation of the latent numbers.
All inputs are finite; a program needn't handle non-finite values.
Results may differ from a plain program's by a relative error of at most 0.014.
The roundings to bfloat16 on the way count: a program that leaves them out, or rounds other values in their place, can miss the bound.
Values may be sent and summed in bfloat16 or wider, within the bound.
No kernel may reach another device: no remote copies, remote signals or barrier semaphores. Data moves between devices by JAX's collectives and lax.ppermute only.
A program may use at most 192 MiB of HBM per device.

v0:
```python
import math
import jax
import jax.numpy as jnp
from jax import lax
from jax.sharding import PartitionSpec as P

D = 384
HEADS = 6
HD = 64
FF = 1536
SEQ = 256
NS_ITERS = 3
LN_EPSILON = 1e-06
MOMENTUM_RATE = 0.95
LEARN_RATE = 0.2
COEFF_A = 3.4445
COEFF_B = -4.775
COEFF_C = 2.0315


def matrix_shapes():
    return [(D, 6 * D), (D, 3 * D), (D, D), (D, FF), (FF, D)]


def unpack(flat_vec):
    pieces = []
    offset = 0
    for rows_count, cols_count in matrix_shapes():
        pieces.append(
            flat_vec[offset : offset + rows_count * cols_count].reshape(rows_count, cols_count)
        )
        offset += rows_count * cols_count
    return pieces


def matmul(lhs_array, rhs_array):
    return jnp.dot(lhs_array, rhs_array, preferred_element_type=jnp.float32)


def contract(pattern, lhs_array, rhs_array):
    return jnp.einsum(pattern, lhs_array, rhs_array, preferred_element_type=jnp.float32)


def modulate(hidden, shifts, scales):
    center = jnp.mean(hidden, axis=-1, keepdims=True)
    spread = jnp.mean(jnp.square(hidden - center), axis=-1, keepdims=True)
    return (hidden - center) * lax.rsqrt(spread + LN_EPSILON) * (1.0 + scales) + shifts


def gelu_tanh(values_in):
    return jax.nn.gelu(values_in, approximate=True)


def orthogonalize(matrix):
    flipped = matrix.shape[0] > matrix.shape[1]
    current = matrix.T if flipped else matrix
    current = current / (jnp.sqrt(jnp.sum(current * current)) + 1e-07)
    for newton_step in range(NS_ITERS):
        square = jnp.dot(current, current.T, precision=lax.Precision.HIGHEST)
        polynomial = COEFF_B * square + COEFF_C * jnp.dot(
            square, square, precision=lax.Precision.HIGHEST
        )
        current = COEFF_A * current + jnp.dot(polynomial, current, precision=lax.Precision.HIGHEST)
    return current.T if flipped else current


def update_scale(rows_count, cols_count):
    return LEARN_RATE * 0.2 * math.sqrt(max(rows_count, cols_count))


def scaled_update(matrix, factor):
    return (factor * orthogonalize(matrix)).reshape(-1)


def empty_update(matrix, factor):
    return jnp.zeros((matrix.shape[0] * matrix.shape[1],), jnp.float32)


def forward_pass(tokens, cond_rows, weights):
    adaln_weight, qkv_weight, out_weight, up_weight, down_weight = weights
    batch_size = tokens.shape[0]
    row_count = batch_size * SEQ
    silu_cond = jax.nn.silu(cond_rows.astype(jnp.float32)).astype(jnp.bfloat16)
    modulation = matmul(silu_cond, adaln_weight).reshape(batch_size, 6, 1, D)
    mod_parts = tuple((modulation[:, position] for position in range(6)))
    shift_attn, scale_attn, gate_attn, shift_mlp, scale_mlp, gate_mlp = mod_parts
    residual = tokens.astype(jnp.float32)
    attn_input = modulate(residual, shift_attn, scale_attn).astype(jnp.bfloat16)
    qkv_all = matmul(attn_input.reshape(row_count, D), qkv_weight).astype(jnp.bfloat16)
    qkv_heads = qkv_all.reshape(batch_size, SEQ, 3, HEADS, HD).transpose(2, 0, 3, 1, 4)
    queries, key_vecs, value_vecs = (qkv_heads[0], qkv_heads[1], qkv_heads[2])
    scores = contract("bhqd,bhkd->bhqk", queries, key_vecs) * HD ** (-0.5)
    log_total = jax.nn.logsumexp(scores, axis=-1, keepdims=True)
    attn_probs = jnp.exp(scores - log_total).astype(jnp.bfloat16)
    attn_mixed = contract("bhqk,bhkd->bhqd", attn_probs, value_vecs).astype(jnp.bfloat16)
    attn_mixed = attn_mixed.transpose(0, 2, 1, 3).reshape(row_count, D)
    attn_out = matmul(attn_mixed, out_weight).reshape(batch_size, SEQ, D)
    after_attn = residual + gate_attn * attn_out
    mlp_input = (
        modulate(after_attn, shift_mlp, scale_mlp).astype(jnp.bfloat16).reshape(row_count, D)
    )
    pre_act = matmul(mlp_input, up_weight)
    activated = gelu_tanh(pre_act).astype(jnp.bfloat16)
    mlp_out = matmul(activated, down_weight).reshape(batch_size, SEQ, D)
    blended = (after_attn + gate_mlp * mlp_out).astype(jnp.bfloat16)
    kept_state = (
        silu_cond,
        mod_parts,
        residual,
        attn_input,
        queries,
        key_vecs,
        value_vecs,
        log_total,
        attn_mixed,
        attn_out,
        after_attn,
        mlp_input,
        pre_act,
        activated,
        mlp_out,
    )
    return (blended, kept_state)


def backward_pass(kept_state, weights, cotangent):
    (
        silu_cond,
        mod_parts,
        residual,
        attn_input,
        queries,
        key_vecs,
        value_vecs,
        log_total,
        attn_mixed,
        attn_out,
        after_attn,
        mlp_input,
        pre_act,
        activated,
        mlp_out,
    ) = kept_state
    adaln_weight, qkv_weight, out_weight, up_weight, down_weight = weights
    shift_attn, scale_attn, gate_attn, shift_mlp, scale_mlp, gate_mlp = mod_parts
    batch_size = cotangent.shape[0]
    row_count = batch_size * SEQ
    upstream = cotangent.astype(jnp.float32)
    grad_gate_mlp = jnp.sum(upstream * mlp_out, axis=1, keepdims=True)
    grad_mlp_out = (upstream * gate_mlp).astype(jnp.bfloat16).reshape(row_count, D)
    grad_down = matmul(activated.T, grad_mlp_out)
    grad_act = matmul(grad_mlp_out, down_weight.T)
    grad_pre = jax.vjp(gelu_tanh, pre_act)[1](grad_act)[0].astype(jnp.bfloat16)
    grad_up = matmul(mlp_input.T, grad_pre)
    grad_mlp_in = matmul(grad_pre, up_weight.T).reshape(batch_size, SEQ, D)
    grad_after, grad_shift_mlp, grad_scale_mlp = jax.vjp(
        modulate, after_attn, shift_mlp, scale_mlp
    )[1](grad_mlp_in)
    grad_after = upstream + grad_after
    grad_gate_attn = jnp.sum(grad_after * attn_out, axis=1, keepdims=True)
    grad_attn_out = (grad_after * gate_attn).astype(jnp.bfloat16).reshape(row_count, D)
    grad_outw = matmul(attn_mixed.T, grad_attn_out)
    grad_mixed = matmul(grad_attn_out, out_weight.T).astype(jnp.bfloat16)
    grad_mixed = grad_mixed.reshape(batch_size, SEQ, HEADS, HD).transpose(0, 2, 1, 3)
    scores = contract("bhqd,bhkd->bhqk", queries, key_vecs) * HD ** (-0.5)
    probs_full = jnp.exp(scores - log_total)
    grad_values = contract("bhqk,bhqd->bhkd", probs_full.astype(jnp.bfloat16), grad_mixed)
    grad_probs = contract("bhqd,bhkd->bhqk", grad_mixed, value_vecs)
    row_dots = jnp.sum(probs_full * grad_probs, axis=-1, keepdims=True)
    grad_scores = (probs_full * (grad_probs - row_dots) * HD ** (-0.5)).astype(jnp.bfloat16)
    grad_queries = contract("bhqk,bhkd->bhqd", grad_scores, key_vecs)
    grad_keys = contract("bhqk,bhqd->bhkd", grad_scores, queries)
    grad_qkv = jnp.stack([grad_queries, grad_keys, grad_values], axis=0).transpose(1, 3, 0, 2, 4)
    grad_qkv = grad_qkv.reshape(row_count, 3 * D).astype(jnp.bfloat16)
    grad_qkvw = matmul(attn_input.reshape(row_count, D).T, grad_qkv)
    grad_attn_in = matmul(grad_qkv, qkv_weight.T).reshape(batch_size, SEQ, D)
    grad_resid, grad_shift_attn, grad_scale_attn = jax.vjp(
        modulate, residual, shift_attn, scale_attn
    )[1](grad_attn_in)
    grad_tokens = grad_after + grad_resid
    grad_mod = jnp.concatenate(
        [
            grad_shift_attn,
            grad_scale_attn,
            grad_gate_attn,
            grad_shift_mlp,
            grad_scale_mlp,
            grad_gate_mlp,
        ],
        axis=1,
    )
    grad_mod = grad_mod.reshape(batch_size, 6 * D).astype(jnp.bfloat16)
    grad_adaln = matmul(silu_cond.T, grad_mod)
    flat_grads = jnp.concatenate(
        [
            grad_adaln.reshape(-1),
            grad_qkvw.reshape(-1),
            grad_outw.reshape(-1),
            grad_up.reshape(-1),
            grad_down.reshape(-1),
        ]
    )
    return (grad_tokens, flat_grads)


def on_device(tokens, conditions, assignment, params, momentum, cotangent):
    cond_table = lax.all_gather(conditions, ("fsdp", "rep"), axis=0, tiled=True)
    cond_rows = jnp.take(cond_table, assignment, axis=0)
    low_params = params.astype(jnp.bfloat16)
    gathered = lax.all_gather(low_params, "fsdp", axis=0, tiled=True)
    blended, kept_state = forward_pass(tokens, cond_rows, unpack(gathered))
    back_flat = lax.all_gather(low_params, "fsdp", axis=0, tiled=True)
    grad_tokens, flat_grads = backward_pass(kept_state, unpack(back_flat), cotangent)
    group_part = lax.psum_scatter(flat_grads, "fsdp", scatter_dimension=0, tiled=True)
    full_grad = lax.psum(group_part, "rep")
    new_momentum = MOMENTUM_RATE * momentum + full_grad
    whole_mom = lax.all_gather(new_momentum, "fsdp", axis=0, tiled=True)
    fsdp_rank = lax.axis_index("fsdp")
    group_size = lax.axis_size("fsdp")
    shard_len = params.shape[0]
    updates = []
    offset = 0
    for rows_count, cols_count in matrix_shapes():
        length = rows_count * cols_count
        piece = whole_mom[offset : offset + length].reshape(rows_count, cols_count)
        factor = jnp.float32(update_scale(rows_count, cols_count))
        owner_rank = (offset // shard_len + group_size // 2) % group_size
        updates.append(
            lax.cond(fsdp_rank == owner_rank, scaled_update, empty_update, piece, factor)
        )
        offset += length
    local_update = lax.psum_scatter(
        jnp.concatenate(updates), "fsdp", scatter_dimension=0, tiled=True
    )
    new_params = params - local_update
    return (blended, grad_tokens, full_grad, new_params, new_momentum)


def solution(mesh):
    in_specs = (
        P(("fsdp", "rep"), None, None),
        P(("fsdp", "rep"), None),
        P(("fsdp", "rep")),
        P("fsdp"),
        P("fsdp"),
        P(("fsdp", "rep"), None, None),
    )
    out_specs = (
        P(("fsdp", "rep"), None, None),
        P(("fsdp", "rep"), None, None),
        P("fsdp"),
        P("fsdp"),
        P("fsdp"),
    )
    return jax.shard_map(
        on_device, mesh=mesh, in_specs=in_specs, out_specs=out_specs, check_vma=False
    )
```

profile of v0, /device:TPU:0, one launch (start us, length us, event | category | flops | bytes accessed | tf_op | source)
XLA Modules:
  0.0 911.6 jit_solution(14796318998570174122)
XLA Ops:
  7.2 3.0 convert_element_type.90
  10.3 44.1 %all-gather = bf16[32,2,384]{2,1,0:T(2,128)(2,1)S(1)} all-gather(bf16[1,2,384]{2,1,0:T(2,128)(2,1)S(1)} %bitcast.245), channel_id=1, replica_groups=mesh['fsdp'=4,'rep'=8] {'fsdp','rep'}, dimensions={0}, use_global_device_ids=true | all-gather | bytes 50688 | tf_op jit(solution)/shard_map/all_gather | solution.py:207
  55.5 19.7 %all-gather.4.cloned.1.call-done = bf16[2654208]{0:T(1024)(128)(2,1)} async-done(((bf16[663552]{0:T(1024)(128)(2,1)}), bf16[2654208]{0:T(1024)(128)(2,1)}) %all-gather.4.cloned.1.call-update) | async-done | bytes 5308432 | tf_op jit(solution)/shard_map/all_gather | solution.py:210
  79.1 2.0 reshape.358
  81.1 2.0 slice.162
  88.2 2.2 reshape.357
  90.4 2.2 slice.172
  92.5 3.0 slice.157
  95.5 2.8 copy.42
  99.5 2.1 fusion.67
  108.5 2.8 fusion.36
  111.2 2.2 fusion.116
  115.5 2.4 fusion.117
  118.0 2.5 fusion.72
  123.3 1.9 copy.47
  127.1 2.5 convolution_bitcast_fusion
  129.6 3.3 fusion.73
  132.9 5.2 fusion.49
  138.1 5.1 fusion.52
  144.6 2.3 copy.55
  153.1 3.4 reshape.341
  158.1 2.5 fusion.68
  164.9 2.1 reshape.337
  167.0 4.1 constant_dynamic-update-slice_fusion.6
  179.8 205.9 %all-reduce.8.cloned.1.call-done = f32[2654208]{0:T(1024)} async-done(((f32[2654208]{0:T(1024)}), f32[2654208]{0:T(1024)}) %all-reduce.8.cloned.1.call-update) | async-done | bytes 10616848
  385.8 3.4 dynamic-slice.1
  389.3 69.3 %all-reduce.6.cloned.1.call-done = f32[663552]{0:T(1024)} async-done(((f32[663552]{0:T(1024)}), f32[663552]{0:T(1024)}) %all-reduce.6.cloned.1.call-update) | async-done | bytes 2654224 | tf_op jit(solution)/shard_map/psum | solution.py:215
  458.5 3.6 multiply_add_fusion.3
  462.2 105.5 %all-gather.6.cloned.1.call-done = f32[2654208]{0:T(1024)} async-done(((f32[663552]{0:T(1024)}), f32[2654208]{0:T(1024)}) %all-gather.6.cloned.1.call-update) | async-done | bytes 10616848 | tf_op jit(solution)/shard_map/all_gather | solution.py:217
  567.7 9.3 %conditional.5 = (f32[884736]{0:T(1024)S(1)}) conditional(s32[]{:T(128)} %convert_element_type.110, () %tuple.38, f32[2654208]{0:T(1024)} %all-gather.6.cloned.1.call-done), branch_computations={%region_21.22_spmd, %region_22.24_spmd} | conditional | flops 26509787136 | bytes 63701028 | solution.py:229
  577.0 2.1 constant_dynamic-update-slice_fusion.7
  579.1 14.8 %conditional.6 = (f32[442368]{0:T(1024)S(1)}) conditional(s32[]{:T(128)} %convert_element_type.111, () %tuple.39, f32[2654208]{0:T(1024)} %all-gather.6.cloned.1.call-done), branch_computations={%region_24.25_spmd, %region_25.27_spmd} | conditional | flops 14274772992 | bytes 35389476 | solution.py:229
  595.3 15.7 %conditional.7 = (f32[147456]{0:T(1024)S(1)}) conditional(s32[]{:T(128)} %convert_element_type.112, () %tuple.40, f32[2654208]{0:T(1024)} %all-gather.6.cloned.1.call-done), branch_computations={%region_27.28_spmd, %region_28.30_spmd} | conditional | flops 6118096896 | bytes 16515108 | solution.py:229
  611.8 41.5 %conditional.8 = (f32[589824]{0:T(1024)S(1)}) conditional(s32[]{:T(128)} %convert_element_type.112, () %tuple.41, f32[2654208]{0:T(1024)} %all-gather.6.cloned.1.call-done), branch_computations={%region_30.31_spmd, %region_31.33_spmd} | conditional | flops 18353111040 | bytes 44826660 | solution.py:229
  611.8 2.9 multiply_reduce_fusion.3
  615.4 3.2 slice_divide_fusion.3
  618.6 2.4 div.75
  621.1 4.0 fusion.109
  626.3 4.0 convolution_add_fusion.11
  630.3 4.2 fusion.110
  635.8 4.0 convolution_add_fusion.10
  639.8 4.0 fusion.111
  645.1 5.5 fusion.12
  650.6 2.3 reshape.307
  655.0 10.3 %conditional.9 = (f32[589824]{0:T(1024)S(1)}) conditional(s32[]{:T(128)} %convert_element_type.113, () %tuple.42, f32[2654208]{0:T(1024)} %all-gather.6.cloned.1.call-done), branch_computations={%region_33.34_spmd, %region_34.36_spmd} | conditional | flops 18360188928 | bytes 110887024 | solution.py:229
  668.1 2.6 fusion.65
  670.7 228.7 %all-reduce.10.cloned.1.call-done = f32[2654208]{0:T(1024)} async-done(((f32[2654208]{0:T(1024)}), f32[2654208]{0:T(1024)}) %all-reduce.10.cloned.1.call-update) | async-done | bytes 10616848
  899.5 3.7 dynamic-slice_subtract_fusion
  (215 shorter events, 73.5 us)
Async XLA Ops:
  7.2 3.1 copy-start.55
  7.2 47.2 %copy-start.58 = (s32[2]{0:T(128)S(1)}, s32[2]{0:T(128)}, u32[]{:S(2)}) copy-start(s32[2]{0:T(128)} %param.18) | copy-start | bytes 28
  7.2 47.8 %copy-start.3 = (bf16[2,256,384]{2,1,0:T(8,128)(2,1)S(1)}, bf16[2,256,384]{2,1,0:T(8,128)(2,1)}, u32[]{:S(2)}) copy-start(bf16[2,256,384]{2,1,0:T(8,128)(2,1)} %param.16) | copy-start | bytes 1179652
  7.2 68.0 %all-gather.4.cloned.1.call-start = ((), (), s32[]{:S(2)}) async-start(), calls=%async_computation | async-start | bytes 6635520 | tf_op jit(solution)/shard_map/all_gather | solution.py:210
  10.3 375.5 %all-reduce.8.cloned.1.call-start = ((), (), s32[]{:S(2)}) async-start(), calls=%async_computation.3 | async-start | bytes 21233664
  55.0 43.3 %copy-start.46 = (bf16[2,384]{1,0:T(2,128)(2,1)}, bf16[2,384]{1,0:T(2,128)(2,1)S(1)}, u32[]{:S(2)}) copy-start(bf16[2,384]{1,0:T(2,128)(2,1)S(1)} %gather_fusion) | copy-start | bytes 4612
  55.2 44.3 %copy-start.34 = (f32[2,256]{1,0:T(2,128)}, f32[2,256]{1,0:T(2,128)S(1)}, u32[]{:S(2)}) copy-start(f32[2,256]{1,0:T(2,128)S(1)} %broadcast_multiply_fusion.2) | copy-start | bytes 6148
  55.5 25.6 %copy-start.42 = (f32[2,256]{1,0:T(2,128)}, f32[2,256]{1,0:T(2,128)S(1)}, u32[]{:S(2)}) copy-start(f32[2,256]{1,0:T(2,128)S(1)} %fusion.69) | copy-start | bytes 6148
  55.5 42.8 %copy-start.52 = (pred[2]{0:T(512)(128)(4,1)}, pred[2]{0:T(512)(128)(4,1)S(1)}, u32[]{:S(2)}) copy-start(pred[2]{0:T(512)(128)(4,1)S(1)} %compare_and_fusion) | copy-start | bytes 10
  55.5 44.0 %copy-start.44 = (f32[2,256]{1,0:T(2,128)}, f32[2,256]{1,0:T(2,128)S(1)}, u32[]{:S(2)}) copy-start(f32[2,256]{1,0:T(2,128)S(1)} %fusion.85) | copy-start | bytes 6148
  90.3 2.2 slice-start
  98.2 3.3 copy-start.15
  99.5 3.5 copy-start.37
  99.5 3.5 copy-start.39
  101.6 1.5 copy-start.16
  105.5 2.9 copy-start.20
  105.5 1.4 copy-start.30
  107.0 1.5 copy-start.26
  107.0 1.5 copy-start.29
  111.2 2.2 copy-start.28
  115.5 2.5 copy-start.14
  115.5 2.5 copy-start.25
  115.5 2.4 copy-start.38
  118.0 4.2 copy-start.32
  127.1 2.5 copy-start.22
  144.6 3.4 copy-start.21
  146.9 1.6 copy-start.19
  148.0 3.6 copy-start.2
  153.1 3.5 copy-start.13
  156.6 1.5 copy-start.33
  156.6 1.5 copy-start.35
  156.6 1.5 copy-start.40
  156.6 1.5 copy-start.45
  158.1 2.5 copy-start.17
  161.4 1.4 copy-start.51
  161.4 1.4 copy-start.57
  161.4 1.4 copy-start.56
  161.4 1.4 copy-start.50
  161.4 2.0 copy-start.47
  167.0 4.1 copy-start.10
  171.1 2.7 copy-start.8
  173.8 2.5 copy-start.7
  178.0 280.6 %all-reduce.6.cloned.1.call-start = ((), (), s32[]{:S(2)}) async-start(), calls=%async_computation.1 | async-start | bytes 5308416 | tf_op jit(solution)/shard_map/psum | solution.py:215
  389.2 69.3 %copy-start.23 = (f32[663552]{0:T(1024)S(1)}, f32[663552]{0:T(1024)}, u32[]{:S(2)}) copy-start(f32[663552]{0:T(1024)} %param.20) | copy-start | bytes 7962628
  389.2 178.5 %all-gather.6.cloned.1.call-start = ((), (), s32[]{:S(2)}) async-start(), calls=%async_computation.2 | async-start | bytes 13271040 | tf_op jit(solution)/shard_map/all_gather | solution.py:217
  462.1 437.3 %all-reduce.10.cloned.1.call-start = ((), (), s32[]{:S(2)}) async-start(), calls=%async_computation.4 | async-start | bytes 21233664
  666.8 232.6 %copy-start.5 = (f32[663552]{0:T(1024)S(1)}, f32[663552]{0:T(1024)}, u32[]{:S(2)}) copy-start(f32[663552]{0:T(1024)} %param.19) | copy-start | bytes 7962628
  899.5 3.7 copy-start.6
  (15 other events, 14.5 us)
Sparse Core Ops, SparseCore 0:
  10.4 64.7 all-gather.3
  178.1 207.6 all-reduce.7
  389.3 69.1 all-reduce.5
  462.2 105.4 all-gather.5
  667.0 232.4 all-reduce.9
where the time goes:
time: 916 us; the launch traced here: 912 us
  waiting for transfers between devices  629 us (69%)
  matrix products  80.4 us (9%)
  local copies, waits for them, and re-layouts  77.9 us (9%)
  blocking collectives  44.1 us (5%)
  loops' own time  36.2 us (4%)
  other arithmetic  28.1 us (3%)
  between operations  15.4 us (2%)
    unnamed x7, waiting for transfers between devices  435 us
    all_gather x1, waiting for transfers between devices, on_device(): whole_mom = lax.all_gather(new_momentum, 'fsdp', axis=0, tiled=True)  106 us
    psum x1, waiting for transfers between devices, on_device(): full_grad = lax.psum(group_part, 'rep')  69.3 us
    all_gather x1, blocking collectives, on_device(): cond_table = lax.all_gather(conditions, ('fsdp', 'rep'), axis=0, tiled=True)  44.1 us
    another operation x5, loops' own time, on_device(): lax.cond(fsdp_rank == owner_rank, scaled_update, empty_update, piece, fac...  36.2 us
    unnamed x133, local copies, waits for them, and re-layouts  26.7 us
    dot_general x14, matrix products, matmul(): return jnp.dot(lhs_array, rhs_array, preferred_element_type=jnp.float32)  22 us
    slice x14, local copies, waits for them, and re-layouts, unpack(): flat_vec[offset:offset + rows_count * cols_count]  20.3 us
  transfers between devices with their start and end apart: 5, of which 5 were waited for; matrix products, arithmetic and copies ran while one was open for 0% of the time, Pallas kernels for 0%

commit v1 on v0

--- a/solution.py
+++ b/solution.py
@@ -212,7 +212,7 @@
     back_flat = lax.all_gather(low_params, "fsdp", axis=0, tiled=True)
     grad_tokens, flat_grads = backward_pass(kept_state, unpack(back_flat), cotangent)
     group_part = lax.psum_scatter(flat_grads, "fsdp", scatter_dimension=0, tiled=True)
-    full_grad = lax.psum(group_part, "rep")
+    full_grad = jnp.sum(lax.all_gather(group_part, "rep"), axis=0)
     new_momentum = MOMENTUM_RATE * momentum + full_grad
     whole_mom = lax.all_gather(new_momentum, "fsdp", axis=0, tiled=True)
     fsdp_rank = lax.axis_index("fsdp")

time: 916 us -> 1090 us (1.19)
  waiting for transfers between devices: 629 us -> 738 us
  other arithmetic: 28.1 us -> 57.3 us
  local copies, waits for them, and re-layouts: 77.9 us -> 102 us
    all_gather x0 -> x1, waiting for transfers between devices: none -> 188 us  [on_device(): full_grad = jnp.sum(lax.all_gather(group_part, 'rep'), axis=0)]
    psum x1 -> x0, waiting for transfers between devices: 69.3 us -> none  [on_device(): full_grad = lax.psum(group_part, 'rep')]
    reduce_sum x0 -> x1, other arithmetic: none -> 29.4 us  [on_device(): full_grad = jnp.sum(lax.all_gather(group_part, 'rep'), axis=0)]
    all_gather x0 -> x1, local copies, waits for them, and re-layouts: none -> 17.9 us  [on_device(): full_grad = jnp.sum(lax.all_gather(group_part, 'rep'), axis=0)]
    slice x14 -> x13, local copies, waits for them, and re-layouts: 20.3 us -> 23.4 us  [unpack(): flat_vec[offset:offset + rows_count * cols_count]]
    unnamed x133 -> x136, local copies, waits for them, and re-layouts: 26.7 us -> 26 us
where the time goes in v1:
time: 1090 us; the launch traced here: 1080 us
  waiting for transfers between devices  738 us (68%)
  local copies, waits for them, and re-layouts  102 us (9%)
  matrix products  82.2 us (8%)
  other arithmetic  57.3 us (5%)
  loops' own time  44.3 us (4%)
  blocking collectives  44.1 us (4%)
  between operations  15.7 us (1%)
    unnamed x7, waiting for transfers between devices  426 us
    all_gather x1, waiting for transfers between devices, on_device(): full_grad = jnp.sum(lax.all_gather(group_part, 'rep'), axis=0)  188 us
    all_gather x1, waiting for transfers between devices, on_device(): whole_mom = lax.all_gather(new_momentum, 'fsdp', axis=0, tiled=True)  104 us
    another operation x5, loops' own time, on_device(): lax.cond(fsdp_rank == owner_rank, scaled_update, empty_update, piece, fac...  44.3 us
    all_gather x1, blocking collectives, on_device(): cond_table = lax.all_gather(conditions, ('fsdp', 'rep'), axis=0, tiled=True)  44.1 us
    reduce_sum x1, other arithmetic, on_device(): full_grad = jnp.sum(lax.all_gather(group_part, 'rep'), axis=0)  29.4 us
    unnamed x136, local copies, waits for them, and re-layouts  26 us
    dot_general x14, matrix products, matmul(): return jnp.dot(lhs_array, rhs_array, preferred_element_type=jnp.float32)  23.6 us
  transfers between devices with their start and end apart: 5, of which 5 were waited for; matrix products, arithmetic and copies ran while one was open for 0% of the time, Pallas kernels for 0%

profile of v1, /device:TPU:0, one launch (start us, length us, event | category | flops | bytes accessed | tf_op | source)
XLA Modules:
  0.0 1083.4 jit_solution(2894275211151539979)
XLA Ops:
  7.2 3.0 convert_element_type.90
  10.3 44.1 %all-gather.1 = bf16[32,2,384]{2,1,0:T(2,128)(2,1)S(1)} all-gather(bf16[1,2,384]{2,1,0:T(2,128)(2,1)S(1)} %bitcast.245), channel_id=1, replica_groups=mesh['fsdp'=4,'rep'=8] {'fsdp','rep'}, dimensions={0}, use_global_device_ids=true | all-gather | bytes 50688 | tf_op jit(solution)/shard_map/all_gather | solution.py:207
  55.5 19.7 %all-gather.6.cloned.1.call-done = bf16[2654208]{0:T(1024)(128)(2,1)} async-done(((bf16[663552]{0:T(1024)(128)(2,1)}), bf16[2654208]{0:T(1024)(128)(2,1)}) %all-gather.6.cloned.1.call-update) | async-done | bytes 5308432 | tf_op jit(solution)/shard_map/all_gather | solution.py:210
  86.8 2.8 slice.177
  89.6 3.6 slice.157
  93.1 2.2 copy.61
  104.5 2.9 reshape.328
  112.5 2.8 fusion.36
  117.5 2.5 fusion.72
  126.7 2.5 convolution_bitcast_fusion
  129.2 3.3 fusion.73
  132.4 5.1 fusion.52
  137.6 5.2 fusion.49
  142.8 3.3 reshape.359
  147.5 2.2 copy.74
  149.8 2.2 fusion.116
  153.2 2.5 fusion.68
  155.9 2.5 fusion.95
  158.4 4.6 reshape.337
  163.0 4.1 constant_dynamic-update-slice_fusion.6
  170.0 2.6 reshape.338
  173.5 3.2 reshape.341
  178.2 3.0 constant_dynamic-update-slice_fusion.14
  188.1 205.9 %all-reduce.5.cloned.1.call-done = f32[2654208]{0:T(1024)} async-done(((f32[2654208]{0:T(1024)}), f32[2654208]{0:T(1024)}) %all-reduce.5.cloned.1.call-update) | async-done | bytes 10616848
  394.0 3.4 dynamic-slice.1
  397.7 187.5 %all-gather.10.cloned.1.call-done = f32[5308416]{0:T(1024)} async-done(((f32[663552]{0:T(1024)}), f32[5308416]{0:T(1024)}) %all-gather.10.cloned.1.call-update) | async-done | bytes 21233680 | tf_op jit(solution)/shard_map/all_gather | solution.py:215
  585.2 17.9 %reshape.351 = f32[8,663552]{1,0:T(8,128)} reshape(f32[5308416]{0:T(1024)} %all-gather.10.cloned.1.call-done) | data formatting | bytes 42467328 | tf_op jit(solution)/shard_map/all_gather | solution.py:215
  603.1 29.4 %reduce_sum.266 = f32[663552]{0:T(1024)S(1)} reduce(f32[8,663552]{1,0:T(8,128)} %reshape.351, f32[]{:T(128)} %constant.97.clone.1), dimensions={0}, to_apply=%region_20.21 | reduce | flops 4644864 | bytes 23887876 | tf_op jit(solution)/shard_map/reduce_sum | solution.py:215
  632.5 4.5 multiply_add_fusion.3
  637.1 104.3 %all-gather.8.cloned.1.call-done = f32[2654208]{0:T(1024)} async-done(((f32[663552]{0:T(1024)}), f32[2654208]{0:T(1024)}) %all-gather.8.cloned.1.call-update) | async-done | bytes 10616848 | tf_op jit(solution)/shard_map/all_gather | solution.py:217
  741.4 9.3 conditional.5
  752.8 14.7 %conditional.6 = (f32[442368]{0:T(1024)S(1)}) conditional(s32[]{:T(128)} %convert_element_type.111, () %tuple.39, f32[2654208]{0:T(1024)} %all-gather.8.cloned.1.call-done), branch_computations={%region_24.25_spmd, %region_25.27_spmd} | conditional | flops 14274772992 | bytes 35389476 | solution.py:229
  768.8 24.7 %conditional.7 = (f32[147456]{0:T(1024)S(1)}) conditional(s32[]{:T(128)} %convert_element_type.112, () %tuple.40, f32[2654208]{0:T(1024)} %all-gather.8.cloned.1.call-done), branch_computations={%region_27.28_spmd, %region_28.30_spmd} | conditional | flops 6118096896 | bytes 16515108 | solution.py:229
  794.4 41.5 %conditional.8 = (f32[589824]{0:T(1024)S(1)}) conditional(s32[]{:T(128)} %convert_element_type.112, () %tuple.41, f32[2654208]{0:T(1024)} %all-gather.8.cloned.1.call-done), branch_computations={%region_30.31_spmd, %region_31.33_spmd} | conditional | flops 18353111040 | bytes 44826660 | solution.py:229
  794.4 2.9 multiply_reduce_fusion.3
  797.9 3.2 slice_divide_fusion.3
  801.2 2.4 div.75
  803.6 4.0 fusion.109
  808.9 4.0 convolution_add_fusion.11
  812.9 4.4 fusion.110
  818.6 4.0 convolution_add_fusion.10
  822.6 4.0 fusion.111
  827.9 5.5 fusion.12
  833.4 2.3 reshape.307
  837.5 9.8 conditional.9
  850.1 2.6 fusion.65
  852.7 220.2 %all-reduce.7.cloned.1.call-done = f32[2654208]{0:T(1024)} async-done(((f32[2654208]{0:T(1024)}), f32[2654208]{0:T(1024)}) %all-reduce.7.cloned.1.call-update) | async-done | bytes 10616848
  1072.9 3.5 dynamic-slice_subtract_fusion
  (219 shorter events, 77.7 us)
Async XLA Ops:
  7.2 3.1 copy-start.57
  7.2 47.2 %copy-start.60 = (s32[2]{0:T(128)S(1)}, s32[2]{0:T(128)}, u32[]{:S(2)}) copy-start(s32[2]{0:T(128)} %param.18) | copy-start | bytes 28
  7.2 47.8 %copy-start.3 = (bf16[2,256,384]{2,1,0:T(8,128)(2,1)S(1)}, bf16[2,256,384]{2,1,0:T(8,128)(2,1)}, u32[]{:S(2)}) copy-start(bf16[2,256,384]{2,1,0:T(8,128)(2,1)} %param.16) | copy-start | bytes 1179652
  7.2 68.0 %all-gather.6.cloned.1.call-start = ((), (), s32[]{:S(2)}) async-start(), calls=%async_computation | async-start | bytes 6635520 | tf_op jit(solution)/shard_map/all_gather | solution.py:210
  10.3 383.8 %all-reduce.5.cloned.1.call-start = ((), (), s32[]{:S(2)}) async-start(), calls=%async_computation.3 | async-start | bytes 21233664
  55.0 40.4 %copy-start.49 = (bf16[2,384]{1,0:T(2,128)(2,1)}, bf16[2,384]{1,0:T(2,128)(2,1)S(1)}, u32[]{:S(2)}) copy-start(bf16[2,384]{1,0:T(2,128)(2,1)S(1)} %gather_fusion) | copy-start | bytes 4612
  55.2 45.2 %copy-start.37 = (f32[2,256]{1,0:T(2,128)}, f32[2,256]{1,0:T(2,128)S(1)}, u32[]{:S(2)}) copy-start(f32[2,256]{1,0:T(2,128)S(1)} %broadcast_multiply_fusion.2) | copy-start | bytes 6148
  55.5 21.5 %copy-start.45 = (f32[2,256]{1,0:T(2,128)}, f32[2,256]{1,0:T(2,128)S(1)}, u32[]{:S(2)}) copy-start(f32[2,256]{1,0:T(2,128)S(1)} %fusion.69) | copy-start | bytes 6148
  55.5 39.9 %copy-start.54 = (pred[2]{0:T(512)(128)(4,1)}, pred[2]{0:T(512)(128)(4,1)S(1)}, u32[]{:S(2)}) copy-start(pred[2]{0:T(512)(128)(4,1)S(1)} %compare_and_fusion) | copy-start | bytes 10
  55.5 44.9 %copy-start.47 = (f32[2,256]{1,0:T(2,128)}, f32[2,256]{1,0:T(2,128)S(1)}, u32[]{:S(2)}) copy-start(f32[2,256]{1,0:T(2,128)S(1)} %fusion.85) | copy-start | bytes 6148
  95.4 5.0 copy-start.25
  98.1 3.4 copy-start.40
  98.1 3.4 copy-start.42
  99.3 3.7 copy-start.11
  107.6 1.3 copy-start.13
  109.6 2.9 copy-start.20
  109.6 1.4 copy-start.33
  110.9 1.6 copy-start.23
  111.0 1.5 copy-start.29
  111.0 1.5 copy-start.34
  112.5 5.0 copy-start.5
  112.5 2.8 copy-start.32
  115.3 1.8 copy-start.27
  115.4 2.1 copy-start.15
  115.4 2.1 copy-start.26
  115.4 2.1 copy-start.41
  117.5 4.2 copy-start.35
  126.6 2.5 copy-start.22
  147.4 2.4 copy-start.24
  147.4 2.4 copy-start.28
  149.8 2.2 copy-start.6
  149.8 2.2 copy-start.30
  153.2 2.6 copy-start.53
  153.2 2.6 copy-start.59
  153.2 2.6 copy-start.58
  153.2 2.7 copy-start.52
  153.2 2.7 copy-start.50
  153.2 2.7 copy-start.55
  163.0 4.1 copy-start.14
  170.0 2.6 copy-start.21
  170.0 3.1 copy-start.19
  178.2 3.8 copy-start.10
  182.1 2.5 copy-start.9
  186.3 399.0 %all-gather.10.cloned.1.call-start = ((), (), s32[]{:S(2)}) async-start(), calls=%async_computation.2 | async-start | bytes 23887872 | tf_op jit(solution)/shard_map/all_gather | solution.py:215
  397.5 343.9 %all-gather.8.cloned.1.call-start = ((), (), s32[]{:S(2)}) async-start(), calls=%async_computation.1 | async-start | bytes 13271040 | tf_op jit(solution)/shard_map/all_gather | solution.py:217
  632.5 4.5 copy-start.7
  637.0 435.9 %all-reduce.7.cloned.1.call-start = ((), (), s32[]{:S(2)}) async-start(), calls=%async_computation.4 | async-start | bytes 21233664
  848.9 224.1 %copy-start.8 = (f32[663552]{0:T(1024)S(1)}, f32[663552]{0:T(1024)}, u32[]{:S(2)}) copy-start(f32[663552]{0:T(1024)} %param.19) | copy-start | bytes 7962628
  (16 other events, 15.1 us)
Sparse Core Ops, SparseCore 0:
  10.4 64.7 all-gather.5
  186.4 207.6 all-reduce.4
  397.6 187.5 all-gather.9
  637.2 104.1 all-gather.7
  849.0 223.9 all-reduce.6
